TPU v7x, 512 devices: a whole 4x4x16 slice. The times are simulated.
512 devices in a mesh: stops: 256 (over y, x, z), veh: 2 (over core).
Axes of the slice: x: 4, y: 4, z: 16, core: 2. Of those that a mesh axis runs over, the one named last changes fastest.
Arguments:
- customer_features: bfloat16 [1048576, 128], P('stops'), may hold values from -20 to 20, as said below
- customer_loads: int32 [1048576], P('stops'), may hold values from 1 to 8
- truck_limits: int32 [2048], replicated, may hold values from 1536 to 3072
- truck_features: bfloat16 [2048, 128], replicated, may hold values from -20 to 20
- customer_average_matrix: bfloat16 [128, 128], replicated, may hold values from -1.5 to 1.5
- truck_identity_matrix: bfloat16 [128, 128], replicated, may hold values from -0.5 to 0.5
- hidden_offset: float32 [128], replicated, may hold values from -4 to 4
- output_projector: bfloat16 [128, 128], replicated, may hold values from -0.5 to 0.5
Outputs:
- new_vehicles: bfloat16 [2048, 128], P('veh')
Inputs may be any that keep to these rules, and one draw needn't show every extreme that they name: `customer_features`: stop embeddings; stops of one block of 4096 form one region.
All inputs are finite; a program needn't handle non-finite values.
Results may differ from a plain program's by a relative error of at most 0.0085.
Values may be sent and summed in bfloat16 or wider, within the bound.
No kernel may reach another device: no remote copies, remote signals or barrier semaphores. Data moves between devices by JAX's collectives and lax.ppermute only.
A program may use at most 64 MiB of HBM per device.

v0:
```python
import jax
import jax.numpy as jnp
from jax import lax
from jax.sharding import PartitionSpec as P


def joined(part, axis, combine):
    gathered = jax.tree.map(lambda a: lax.all_gather(a, axis), part)

    def take(source):
        return jax.tree.map(lambda a: lax.dynamic_index_in_dim(a, source, 0, False), gathered)

    return lax.fori_loop(
        1, lax.axis_size(axis), lambda source, state: combine(state, take(source)), take(0)
    )


def join_parts(first, second):
    top = jnp.maximum(first[0], second[0])
    total = first[1] * jnp.exp(first[0] - top) + second[1] * jnp.exp(second[0] - top)
    return (top, total)


def row_lse(values):
    top = jnp.max(values, axis=1)
    total = jnp.sum(jnp.exp(values - top[:, None]), axis=1)
    top, total = joined((top, total), "veh", join_parts)
    return top + jnp.log(total)


def update_rows(
    num,
    den,
    own_rows,
    customer_average_matrix,
    truck_identity_matrix,
    hidden_offset,
    output_projector,
):
    centroid = (num / den[:, None]).astype(jnp.bfloat16)
    pre = jnp.dot(centroid, customer_average_matrix, preferred_element_type=jnp.float32)
    pre = (
        pre
        + jnp.dot(own_rows, truck_identity_matrix, preferred_element_type=jnp.float32)
        + hidden_offset[None, :]
    )
    hidden = jax.nn.silu(pre).astype(jnp.bfloat16)
    update = jnp.dot(hidden, output_projector, preferred_element_type=jnp.float32)
    return (own_rows.astype(jnp.float32) + update).astype(jnp.bfloat16)


def on_device(
    customer_features,
    customer_loads,
    truck_limits,
    truck_features,
    customer_average_matrix,
    truck_identity_matrix,
    hidden_offset,
    output_projector,
):
    width = truck_features.shape[1]
    scale = 1.0 / width**0.5
    veh_count = lax.axis_size("veh")
    truck_index = lax.axis_index("veh")
    radius_span = truck_features.shape[0] // veh_count
    my_veh = lax.dynamic_slice_in_dim(truck_features, truck_index * radius_span, radius_span, 0)
    local_capacity = lax.dynamic_slice_in_dim(
        truck_limits, truck_index * radius_span, radius_span, 0
    )
    log_a = jnp.log(customer_loads.astype(jnp.float32))
    target_share_logarithm = jnp.log(local_capacity.astype(jnp.float32))
    scores = jnp.dot(customer_features, my_veh.T, preferred_element_type=jnp.float32) * scale
    f_one = log_a - row_lse(scores)
    col_part = jnp.sum(jnp.exp(f_one[:, None] + scores), axis=0)
    colsum = lax.psum(col_part, "stops")
    g_one = target_share_logarithm - jnp.log(colsum)
    f_two = log_a - row_lse(scores + g_one[None, :])
    plan = jnp.exp(f_two[:, None] + g_one[None, :] + scores).astype(jnp.bfloat16)
    den = jnp.sum(plan, axis=0, dtype=jnp.float32)
    num = lax.dot_general(
        plan, customer_features, (((0,), (0,)), ((), ())), preferred_element_type=jnp.float32
    )
    num, den = lax.psum((num, den), "stops")
    return update_rows(
        num,
        den,
        my_veh,
        customer_average_matrix,
        truck_identity_matrix,
        hidden_offset,
        output_projector,
    )


def solution(mesh):
    placed = (P("stops", None), P("stops"), P(), P(), P(), P(), P(), P())
    return jax.shard_map(
        on_device, mesh=mesh, in_specs=placed, out_specs=P("veh", None), check_vma=False
    )
```

profile of v0, /device:TPU:32, one launch (start us, length us, event | category | flops | bytes accessed | tf_op | source)
XLA Modules:
  0.0 1458.4 jit_solution(17495390267495161967)
XLA Ops:
  6.5 1.2 copy-done
  7.8 9.0 multiply_reduce_fusion
  16.8 1.8 all-gather
  18.6 8.5 fusion.1
  27.1 1.8 all-gather.1
  29.0 0.0 copy-done.2
  29.0 8.6 fusion.3
  37.6 690.8 %psum.21 = f32[1024]{0:T(1024)S(1)} all-reduce(f32[1024]{0:T(1024)S(1)} %fusion.3), channel_id=1, replica_groups=mesh['stops'=256,'veh'=2] {'stops'}, use_global_device_ids=true, to_apply=%region_3.4 | all-reduce | flops 1024 | bytes 8192 | tf_op jit(solution)/shard_map/psum | solution.py:76
  728.5 7.7 fusion.6
  736.2 7.8 exponential_reduce_fusion
  744.0 1.8 all-gather.2
  745.8 2.0 all-gather.3
  747.9 0.0 copy-start.4
  747.9 0.0 copy-start.1
  747.9 0.0 copy-start.5
  747.9 0.0 copy-start.6
  747.9 0.0 copy-start.7
  747.9 8.5 convert_reduce_fusion
  756.4 3.1 fusion.31
  759.5 0.0 all-reduce.2.cloned.1.call-update
  759.5 689.5 %psum.23 = f32[1024]{0:T(1024)S(1)} all-reduce(f32[1024]{0:T(1024)S(1)} %get-tuple-element.27), channel_id=1, replica_groups=mesh['stops'=256,'veh'=2] {'stops'}, use_global_device_ids=true, to_apply=%region_8.9 | all-reduce | flops 1024 | bytes 8192 | tf_op jit(solution)/shard_map/psum | solution.py:84
  1449.0 0.0 all-reduce.2.cloned.1.call-done
  1449.0 1.4 fusion.11
  1450.4 1.1 fusion.8
  (13 shorter events, 0.1 us)
Async XLA Ops:
  6.5 1.2 copy-start
  6.5 1442.5 %all-reduce.2.cloned.1.call-start = ((), (), s32[]{:S(2)}) async-start(), calls=%async_computation | async-start | bytes 1048576 | tf_op jit(solution)/shard_map/psum | solution.py:84
  7.8 21.2 %copy-start.2 = (s32[4096]{0:T(1024)S(1)}, s32[4096]{0:T(1024)}, u32[]{:S(2)}) copy-start(s32[4096]{0:T(1024)} %param.9) | copy-start | bytes 49156
  18.6 709.8 %copy-start.3 = (s32[2048]{0:T(1024)S(1)}, s32[2048]{0:T(1024)}, u32[]{:S(2)}) copy-start(s32[2048]{0:T(1024)} %param.10) | copy-start | bytes 24580
  747.9 701.2 %copy-start.4 = (bf16[128,128]{1,0:T(8,128)(2,1)S(1)}, bf16[128,128]{1,0:T(8,128)(2,1)}, u32[]{:S(2)}) copy-start(bf16[128,128]{1,0:T(8,128)(2,1)} %param.12) | copy-start | bytes 98308
  747.9 702.5 %copy-start.1 = (bf16[2048,128]{1,0:T(8,128)(2,1)S(1)}, bf16[2048,128]{1,0:T(8,128)(2,1)}, u32[]{:S(2)}) copy-start(bf16[2048,128]{1,0:T(8,128)(2,1)} %param.11) | copy-start | bytes 1572868
  747.9 702.5 %copy-start.5 = (bf16[128,128]{1,0:T(8,128)(2,1)S(1)}, bf16[128,128]{1,0:T(8,128)(2,1)}, u32[]{:S(2)}) copy-start(bf16[128,128]{1,0:T(8,128)(2,1)} %param.15) | copy-start | bytes 98308
  747.9 702.5 %copy-start.6 = (bf16[128,128]{1,0:T(8,128)(2,1)S(1)}, bf16[128,128]{1,0:T(8,128)(2,1)}, u32[]{:S(2)}) copy-start(bf16[128,128]{1,0:T(8,128)(2,1)} %param.13) | copy-start | bytes 98308
  747.9 702.5 %copy-start.7 = (f32[128]{0:T(128)S(1)}, f32[128]{0:T(128)}, u32[]{:S(2)}) copy-start(f32[128]{0:T(128)} %param.14) | copy-start | bytes 1540
Sparse Core Ops, SparseCore 0:
  759.7 383.6 all-reduce.1
where the time goes:
time: 1460 us
  blocking collectives  1390 us (95%)
  other arithmetic  41.2 us (3%)
  matrix products  14.6 us (1%)
    psum x1, blocking collectives, on_device(): colsum = lax.psum(col_part, 'stops')  691 us
    psum x1, blocking collectives, on_device(): num, den = lax.psum((num, den), 'stops')  689 us
  transfers between devices with their start and end apart: 1, of which 0 were waited for; matrix products, arithmetic and copies ran while one was open for 0% of the time, Pallas kernels for 0%

commit v1 on v0

--- a/solution.py
+++ b/solution.py
@@ -2,6 +2,12 @@
 import jax.numpy as jnp
 from jax import lax
 from jax.sharding import PartitionSpec as P
+
+
+def gather_and_add(x, mesh_axis):
+    parts = lax.all_gather(x, mesh_axis, axis=0, tiled=False)
+    total = parts.sum(axis=0)
+    return total
 
 
 def joined(part, axis, combine):
@@ -73,7 +79,7 @@
     scores = jnp.dot(customer_features, my_veh.T, preferred_element_type=jnp.float32) * scale
     f_one = log_a - row_lse(scores)
     col_part = jnp.sum(jnp.exp(f_one[:, None] + scores), axis=0)
-    colsum = lax.psum(col_part, "stops")
+    colsum = gather_and_add(col_part, "stops")
     g_one = target_share_logarithm - jnp.log(colsum)
     f_two = log_a - row_lse(scores + g_one[None, :])
     plan = jnp.exp(f_two[:, None] + g_one[None, :] + scores).astype(jnp.bfloat16)

time: 1460 us -> 961 us (0.66)
  the two profiles are of different devices: /device:TPU:32 before, /device:TPU:0 now
where the time goes in v1:
time: 961 us
  blocking collectives  696 us (72%)
  waiting for transfers between devices  191 us (20%)
  other arithmetic  41.9 us (4%)
  matrix products  14.6 us (2%)
  between operations  13.5 us (1%)
    psum x1, blocking collectives, on_device(): num, den = lax.psum((num, den), 'stops')  689 us
    all_gather x1, waiting for transfers between devices, gather_and_add(): parts = lax.all_gather(x, mesh_axis, axis=0, tiled=False)  191 us
  transfers between devices with their start and end apart: 2, of which 1 were waited for; matrix products, arithmetic and copies ran while one was open for 0% of the time, Pallas kernels for 0%

profile of v1, /device:TPU:0, one launch (start us, length us, event | category | flops | bytes accessed | tf_op | source)
XLA Modules:
  0.0 960.5 jit_solution(4184194626931201981)
XLA Ops:
  6.5 1.2 copy-done
  7.8 9.0 multiply_reduce_fusion
  16.8 1.8 all-gather
  18.6 8.5 fusion.1
  27.1 1.8 all-gather.1
  29.0 9.2 fusion.3
  38.2 0.0 all-gather.7.cloned.1.call-update
  38.3 0.2 all-reduce.2.cloned.1.call-start
  38.5 191.0 %all-gather.7.cloned.1.call-done = f32[262144]{0:T(1024)} async-done(((f32[1024]{0:T(1024)}), f32[262144]{0:T(1024)}) %all-gather.7.cloned.1.call-update) | async-done | bytes 1048592 | tf_op jit(solution)/shard_map/all_gather | solution.py:8
  229.5 1.4 reshape.9
  230.9 0.1 reduce_sum.47
  231.0 7.7 fusion.6
  238.8 7.8 exponential_reduce_fusion
  246.6 1.8 all-gather.3
  248.4 1.8 all-gather.4
  250.3 0.0 copy-start.1
  250.3 0.0 copy-start.5
  250.3 8.5 convert_reduce_fusion
  258.8 3.1 fusion.31
  261.9 0.0 all-reduce.2.cloned.1.call-update
  261.9 689.2 %psum.15 = f32[1024]{0:T(1024)S(1)} all-reduce(f32[1024]{0:T(1024)S(1)} %get-tuple-element.27), channel_id=1, replica_groups=mesh['stops'=256,'veh'=2] {'stops'}, use_global_device_ids=true, to_apply=%region_8.9 | all-reduce | flops 1024 | bytes 8192 | tf_op jit(solution)/shard_map/psum | solution.py:90
  951.1 0.0 all-reduce.2.cloned.1.call-done
  951.2 1.4 fusion.11
  952.6 1.1 fusion.8
  (17 shorter events, 0.1 us)
Async XLA Ops:
  6.5 1.2 copy-start
  6.5 223.0 %all-gather.7.cloned.1.call-start = ((), (), s32[]{:S(2)}) async-start(), calls=%async_computation.1 | async-start | bytes 1052672 | tf_op jit(solution)/shard_map/all_gather | solution.py:8
  7.8 21.2 %copy-start.2 = (s32[4096]{0:T(1024)S(1)}, s32[4096]{0:T(1024)}, u32[]{:S(2)}) copy-start(s32[4096]{0:T(1024)} %param.9) | copy-start | bytes 49156
  18.6 212.4 %copy-start.3 = (s32[2048]{0:T(1024)S(1)}, s32[2048]{0:T(1024)}, u32[]{:S(2)}) copy-start(s32[2048]{0:T(1024)} %param.10) | copy-start | bytes 24580
  38.3 912.9 %all-reduce.2.cloned.1.call-start = ((), (), s32[]{:S(2)}) async-start(), calls=%async_computation | async-start | bytes 1048576 | tf_op jit(solution)/shard_map/psum | solution.py:90
  250.3 700.9 %copy-start.4 = (bf16[128,128]{1,0:T(8,128)(2,1)S(1)}, bf16[128,128]{1,0:T(8,128)(2,1)}, u32[]{:S(2)}) copy-start(bf16[128,128]{1,0:T(8,128)(2,1)} %param.12) | copy-start | bytes 98308
  250.3 702.3 %copy-start.1 = (bf16[2048,128]{1,0:T(8,128)(2,1)S(1)}, bf16[2048,128]{1,0:T(8,128)(2,1)}, u32[]{:S(2)}) copy-start(bf16[2048,128]{1,0:T(8,128)(2,1)} %param.11) | copy-start | bytes 1572868
  250.3 702.3 %copy-start.5 = (bf16[128,128]{1,0:T(8,128)(2,1)S(1)}, bf16[128,128]{1,0:T(8,128)(2,1)}, u32[]{:S(2)}) copy-start(bf16[128,128]{1,0:T(8,128)(2,1)} %param.15) | copy-start | bytes 98308
  250.3 702.3 %copy-start.6 = (bf16[128,128]{1,0:T(8,128)(2,1)S(1)}, bf16[128,128]{1,0:T(8,128)(2,1)}, u32[]{:S(2)}) copy-start(bf16[128,128]{1,0:T(8,128)(2,1)} %param.13) | copy-start | bytes 98308
  250.3 702.3 %copy-start.7 = (f32[128]{0:T(128)S(1)}, f32[128]{0:T(128)}, u32[]{:S(2)}) copy-start(f32[128]{0:T(128)} %param.14) | copy-start | bytes 1540
Sparse Core Ops, SparseCore 0:
  38.4 191.1 all-gather.6
  262.1 388.6 all-reduce.1
